TPU v7x, 256 devices: a whole 4x4x8 slice. The times are simulated.
256 devices in a mesh: ctx: 32 (over x, z_lo, core), head: 2 (over z_hi), tp: 4 (over y).
Axes of the slice: x: 4, y: 4, z: 8 (z_hi: 2, z_lo: 4; z = z_hi * 4 + z_lo), core: 2. Of those that a mesh axis runs over, the one named last changes fastest.
Arguments:
- text_states: bfloat16 [256, 8192], P(None, 'ctx'), may hold values from -6 to 6
- q_weight: bfloat16 [8192, 8192], P('ctx', ('head', 'tp')), may hold values from -0.0625 to 0.0625
- q_gain: float32 [128], replicated, may hold values from 0.1 to 1.9
- visual_key_cache: bfloat16 [16384, 1024], P('ctx', ('head', 'tp')), may hold values from -400 to 400
- visual_value_cache: bfloat16 [16384, 1024], P('ctx', ('head', 'tp')), may hold values from -6 to 6
- block_mask: int32 [256, 64], P(None, 'ctx'), may hold values from 0 to 1, as said below
- lengths: int32 [256], replicated, may hold values from 256 to 16384, as said below
- o_weight: bfloat16 [8192, 8192], P(('head', 'tp'), 'ctx'), may hold values from -0.59765625 to 0.59765625
Outputs:
- updated: bfloat16 [256, 8192], P(('head', 'tp'), 'ctx')
Inputs may be any that keep to these rules, and one draw needn't show every extreme that they name: `block_mask`: segment 0 is visible to every row. `lengths`: some row sees all 16384 tokens.
All inputs are finite; a program needn't handle non-finite values.
Results may differ from a plain program's by a relative error of at most 0.0055.
Values may be sent and summed in bfloat16 or wider, within the bound.
A program may use at most 64 MiB of HBM per device.

v0:
```python
import jax
import jax.numpy as jnp
from jax import lax
from jax.sharding import PartitionSpec as P


def in_blocks(shard, dim, size):
    dims = shard.shape
    parts = shard.reshape(*dims[:dim], size, dims[dim] // size, *dims[dim + 1 :])
    return jnp.moveaxis(parts, dim, 0)


def summed_on_arrival(shard, axis, dim):
    size = lax.axis_size(axis)
    parts = lax.all_to_all(in_blocks(shard, dim, size), axis, 0, 0, tiled=True)
    return jnp.sum(parts, axis=0)


def joined_along(parts, dim):
    parts = jnp.moveaxis(parts, 0, dim)
    dims = parts.shape
    return parts.reshape(*dims[:dim], dims[dim] * dims[dim + 1], *dims[dim + 2 :])


def sent_to_all(shard, axis):
    copies = jnp.broadcast_to(shard, (lax.axis_size(axis), *shard.shape))
    return lax.all_to_all(copies, axis, split_axis=0, concat_axis=0, tiled=True)


def collect(shard, axis, dim):
    return joined_along(sent_to_all(shard, axis), dim)


def over_copies(shard, axis):
    everything = sent_to_all(shard, axis)
    return jnp.max(everything, axis=0)


def side_by_side(arrays, axis, dim, along):
    ends, at = ([], 0)
    for a in arrays[:-1]:
        at += a.shape[along]
        ends.append(at)
    both = jnp.concatenate(arrays, axis=along)
    return tuple(jnp.split(summed_on_arrival(both, axis, dim), ends, axis=along))


def shards(
    text_states,
    q_weight,
    q_gain,
    visual_key_cache,
    visual_value_cache,
    block_mask,
    lengths,
    o_weight,
):
    text_rows = text_states.shape[0]
    columns = q_weight.shape[1]
    head_dim = q_gain.shape[0]
    query_heads = columns // head_dim
    row_block = text_states
    query_share = summed_on_arrival(
        jnp.dot(row_block, q_weight, preferred_element_type=jnp.float32), "ctx", 0
    )
    shaped = query_share.reshape(query_share.shape[0], query_heads, head_dim)
    mean_sq = jnp.mean(shaped * shaped, axis=-1, keepdims=True)
    normed = shaped * lax.rsqrt(mean_sq + 1e-05) * q_gain
    queries = collect(normed.reshape(query_share.shape[0], columns).astype(jnp.bfloat16), "ctx", 0)
    keys_local = visual_key_cache.shape[0]
    segment_len = keys_local // block_mask.shape[1]
    key_block_offset = lax.axis_index("ctx") * keys_local
    positions = key_block_offset + jnp.arange(keys_local, dtype=jnp.int32)
    allowed = (jnp.repeat(block_mask, segment_len, axis=1) == 1) & (
        positions[None, :] < lengths[:, None]
    )
    score_scale = 1.0 / head_dim**0.5
    partial_nums = []
    partial_maxes = []
    partial_totals = []
    for q_head in range(query_heads):
        query_part = queries[:, q_head * head_dim : (q_head + 1) * head_dim]
        scores = (
            lax.dot_general(
                query_part,
                visual_key_cache,
                (((1,), (1,)), ((), ())),
                preferred_element_type=jnp.float32,
            )
            * score_scale
        )
        scores = jnp.where(allowed, scores, jnp.float32(-1e30))
        local_max = jnp.max(scores, axis=1)
        weights = jnp.where(allowed, jnp.exp(scores - local_max[:, None]), jnp.float32(0.0))
        partial_totals.append(jnp.sum(weights, axis=1))
        partial_maxes.append(local_max)
        partial_nums.append(
            jnp.dot(
                weights.astype(jnp.bfloat16), visual_value_cache, preferred_element_type=jnp.float32
            )
        )
    local_num = jnp.concatenate(partial_nums, axis=1)
    local_max = jnp.stack(partial_maxes, axis=1)
    local_total = jnp.stack(partial_totals, axis=1)
    highest = over_copies(local_max, "ctx")
    factor = jnp.exp(local_max - highest)
    scaled_num = local_num * jnp.repeat(factor, head_dim, axis=1)
    scaled_total = local_total * factor
    owned_num, owned_total = side_by_side((scaled_num, scaled_total), "ctx", 0, 1)
    owned = (owned_num / jnp.repeat(owned_total, head_dim, axis=1)).astype(jnp.bfloat16)
    attended = collect(owned, "ctx", 0)
    rows_out = text_rows // lax.axis_size(("head", "tp"))
    row_block = attended
    summed = summed_on_arrival(
        jnp.dot(row_block, o_weight, preferred_element_type=jnp.float32), ("head", "tp"), 0
    )
    residual = lax.dynamic_slice_in_dim(
        text_states, lax.axis_index(("head", "tp")) * rows_out, rows_out, 0
    )
    return (residual.astype(jnp.float32) + summed).astype(jnp.bfloat16)


def solution(mesh):
    in_specs = (
        P(None, "ctx"),
        P("ctx", ("head", "tp")),
        P(),
        P("ctx", ("head", "tp")),
        P("ctx", ("head", "tp")),
        P(None, "ctx"),
        P(),
        P(("head", "tp"), "ctx"),
    )
    out_specs = P(("head", "tp"), "ctx")
    return jax.shard_map(shards, mesh=mesh, in_specs=in_specs, out_specs=out_specs, check_vma=False)
```

profile of v0, /device:TPU:1, one launch (start us, length us, event | category | flops | bytes accessed | tf_op | source)
XLA Modules:
  0.0 180.1 jit_solution(6820126137904986363)
XLA Ops:
  0.0 1.0 copy-done
  1.0 2.2 %convolution_bitcast_fusion = f32[32,8,1024]{2,1,0:T(8,128)} fusion(bf16[256,256]{1,0:T(8,128)(2,1)} %param.8, bf16[256,1024]{1,0:T(8,128)(2,1)S(1)} %copy-done), kind=kOutput, calls=%fused_computation | convolution fusion | flops 134217728 | bytes 1703936 | tf_op jit(solution)/shard_map/dot_general | solution.py:64
  3.2 10.2 %all-to-all-start = ((f32[32,8,1024]{2,1,0:T(8,128)}), f32[32,8,1024]{2,1,0:T(8,128)S(1)}, u32[]{:S(2)}, u32[]{:S(2)}) async-start(f32[32,8,1024]{2,1,0:T(8,128)} %convolution_bitcast_fusion), calls=%async_computation | async-start | bytes 2097152 | tf_op jit(solution)/shard_map/all_to_all | solution.py:15
  13.4 27.8 %all-to-all-done = f32[32,8,1024]{2,1,0:T(8,128)S(1)} async-done(((f32[32,8,1024]{2,1,0:T(8,128)}), f32[32,8,1024]{2,1,0:T(8,128)S(1)}, u32[]{:S(2)}, u32[]{:S(2)}) %all-to-all-start) | async-done | bytes 1048608 | tf_op jit(solution)/shard_map/all_to_all | solution.py:15
  41.3 0.1 reduce_sum.108
  41.4 0.1 bitcast_reduce_fusion
  41.5 0.1 fusion.68
  41.5 0.9 broadcast_in_dim.68
  42.4 3.9 %all-to-all-start.1 = ((bf16[32,8,1024]{2,1,0:T(8,128)(2,1)}), bf16[32,8,1024]{2,1,0:T(8,128)(2,1)S(1)}, u32[]{:S(2)}, u32[]{:S(2)}) async-start(bf16[32,8,1024]{2,1,0:T(8,128)(2,1)} %broadcast_in_dim.68), calls=%async_computation.1 | async-start | bytes 1048576 | tf_op jit(solution)/shard_map/all_to_all | solution.py:27
  46.4 0.2 copy.43
  46.6 16.6 %all-to-all-done.1 = bf16[32,8,1024]{2,1,0:T(8,128)(2,1)S(1)} async-done(((bf16[32,8,1024]{2,1,0:T(8,128)(2,1)}), bf16[32,8,1024]{2,1,0:T(8,128)(2,1)S(1)}, u32[]{:S(2)}, u32[]{:S(2)}) %all-to-all-start.1) | async-done | bytes 524320 | tf_op jit(solution)/shard_map/all_to_all | solution.py:27
  63.2 0.3 fusion.77
  63.5 1.1 fusion.78
  64.6 1.1 fusion.79
  65.6 1.1 fusion.80
  66.7 0.3 fusion.81
  67.0 0.3 fusion.82
  67.4 0.3 fusion.83
  67.7 1.2 fusion.84
  68.9 0.1 stack.66
  69.0 0.7 stack.67
  69.7 0.7 stack.68
  70.3 0.7 stack.69
  71.0 0.7 stack.70
  71.7 0.7 stack.71
  72.4 0.7 stack.72
  73.1 0.7 stack.73
  73.8 2.7 %fusion.32 = (f32[256]{0:T(256)S(1)}, f32[256]{0:T(256)S(1)}, f32[256]{0:T(256)S(1)}, f32[256]{0:T(256)S(1)}, f32[256]{0:T(256)S(1)}, /*index=5*/f32[256]{0:T(256)S(1)}, f32[256]{0:T(256)S(1)}, f32[256]{0:T(256)S(1)}) fusion(f32[256,512]{1,0:T(8,128)S(1)} %get-tuple-element.14, f32[256]{0:T(256)S(1)} %get-tuple-element.13, pred[256,512]{1,0:T(32,128)(4,1)S(1)} %copy.43, ...), kind=kLoop, calls=%fused_computation.59 | loop fusion | flops 3405824 | bytes 4344832 | tf_op jit(solution)/shard_map/reduce_sum | solution.py:95
  76.5 0.1 stack.57
  76.6 0.6 constant_dynamic-update-slice_fusion.7
  77.2 0.7 stack.58
  77.9 0.7 stack.59
  78.6 0.7 stack.60
  79.2 0.7 stack.61
  79.9 0.7 stack.62
  80.6 0.7 stack.63
  81.3 0.7 stack.64
  82.0 0.6 constant_dynamic-update-slice_fusion.15
  82.7 0.7 broadcast_in_dim.79
  83.4 3.7 %all-to-all-start.2 = ((f32[32,256,8]{1,2,0:T(8,128)}), f32[32,256,8]{1,2,0:T(8,128)S(1)}, u32[]{:S(2)}, u32[]{:S(2)}) async-start(f32[32,256,8]{1,2,0:T(8,128)} %broadcast_in_dim.79), calls=%async_computation.2 | async-start | bytes 524288 | tf_op jit(solution)/shard_map/all_to_all | solution.py:27
  87.1 2.1 %fusion.15 = f32[32,8,1024]{2,1,0:T(8,128)} fusion(bf16[512,128]{1,0:T(8,128)(2,1)} %param.12, f32[256,512]{1,0:T(8,128)} %get-tuple-element.16, f32[256]{0:T(256)} %copy-done.28, pred[256,512]{1,0:T(32,128)(4,1)S(1)} %copy.43, s32[512]{0:T(512)} %copy-done.30, s32[256]{0:T(256)} %param.14), kind=kOutput, calls=%fused_computation.33 | convolution fusion | flops 34209792 | bytes 921600 | tf_op jit(solution)/shard_map/dot_general | solution.py:98
  89.2 2.1 %fusion.14 = f32[32,8,1024]{2,1,0:T(8,128)} fusion(f32[32,8,1024]{2,1,0:T(8,128)} %fusion.15, bf16[512,128]{1,0:T(8,128)(2,1)} %param.12, f32[256,512]{1,0:T(8,128)} %get-tuple-element.18, f32[256]{0:T(256)} %copy-done.29, pred[256,512]{1,0:T(32,128)(4,1)S(1)} %copy.43, s32[512]{0:T(512)} %copy-done.30, s32[256]{0:T(256)} %param.14), kind=kOutput, calls=%fused_computation.31 | convolution fusion | flops 34209792 | bytes 921600 | tf_op jit(solution)/shard_map/dot_general | solution.py:98
  91.4 1.0 fusion.13
  92.4 1.0 fusion.12
  93.5 1.0 fusion.11
  94.6 1.0 fusion.10
  95.9 1.0 fusion.9
  96.9 1.0 fusion.8
  97.9 0.6 all-to-all-done.2
  98.5 0.1 reduce_max.92
  98.6 0.1 copy.45
  98.8 0.1 copy.44
  98.9 0.3 broadcast_in_dim.80
  99.2 0.2 reshape.93
  99.4 1.4 mul.91
  100.8 0.1 pad_maximum_fusion
  100.9 38.0 %all_to_all.30 = f32[32,8,1032]{2,1,0:T(8,128)S(1)} all-to-all(f32[32,8,1032]{2,1,0:T(8,128)S(1)} %pad_maximum_fusion), channel_id=1, replica_groups=mesh['ctx'=32,'head'=2,'tp'=4] {'ctx'}, dimensions={0} | all-to-all | bytes 2113536 | tf_op jit(solution)/shard_map/all_to_all | solution.py:15
  138.9 0.1 copy.46
  139.0 0.1 fusion.66
  139.2 20.3 %all_to_all.31 = bf16[32,8,1024]{2,1,0:T(8,128)(2,1)S(1)} all-to-all(bf16[32,8,1024]{2,1,0:T(8,128)(2,1)S(1)} %broadcast_in_dim.82), channel_id=1, replica_groups=mesh['ctx'=32,'head'=2,'tp'=4] {'ctx'}, dimensions={0} | all-to-all | bytes 1048576 | tf_op jit(solution)/shard_map/all_to_all | solution.py:27
  159.5 1.0 fusion.16
  160.5 8.1 %all-to-all-start.5 = ((f32[8,32,256]{2,1,0:T(8,128)}), f32[8,32,256]{2,1,0:T(8,128)S(1)}, u32[]{:S(2)}, u32[]{:S(2)}) async-start(f32[8,32,256]{2,1,0:T(8,128)} %fusion.16), calls=%async_computation.5 | async-start | bytes 524288 | tf_op jit(solution)/shard_map/all_to_all | solution.py:15
  168.6 10.1 %all-to-all-done.5 = f32[8,32,256]{2,1,0:T(8,128)S(1)} async-done(((f32[8,32,256]{2,1,0:T(8,128)}), f32[8,32,256]{2,1,0:T(8,128)S(1)}, u32[]{:S(2)}, u32[]{:S(2)}) %all-to-all-start.5) | async-done | bytes 262176 | tf_op jit(solution)/shard_map/all_to_all | solution.py:15
  178.7 1.3 add_convert_fusion
  (101 shorter events, 0.5 us)
Async XLA Ops:
  0.0 1.0 copy-start
  3.2 10.2 %copy-start.35 = (f32[128]{0:T(128)S(1)}, f32[128]{0:T(128)}, u32[]{:S(2)}) copy-start(f32[128]{0:T(128)} %param.10) | copy-start | bytes 1540
  3.2 38.0 %all-to-all-start = ((f32[32,8,1024]{2,1,0:T(8,128)}), f32[32,8,1024]{2,1,0:T(8,128)S(1)}, u32[]{:S(2)}, u32[]{:S(2)}) async-start(f32[32,8,1024]{2,1,0:T(8,128)} %convolution_bitcast_fusion), calls=%async_computation | async-start | bytes 2097152 | tf_op jit(solution)/shard_map/all_to_all | solution.py:15
  13.4 32.9 %copy-start.32 = (s32[256,2]{0,1:T(2,128)S(1)}, s32[256,2]{0,1:T(2,128)}, u32[]{:S(2)}) copy-start(s32[256,2]{0,1:T(2,128)} %param.13) | copy-start | bytes 6148
  41.3 21.9 %copy-start.33 = (s32[256]{0:T(256)S(1)}, s32[256]{0:T(256)}, u32[]{:S(2)}) copy-start(s32[256]{0:T(256)} %param.14) | copy-start | bytes 3076
  41.4 21.8 %copy-start.36 = (bf16[512,128]{1,0:T(8,128)(2,1)S(1)}, bf16[512,128]{1,0:T(8,128)(2,1)}, u32[]{:S(2)}) copy-start(bf16[512,128]{1,0:T(8,128)(2,1)} %param.11) | copy-start | bytes 393220
  42.4 20.8 %all-to-all-start.1 = ((bf16[32,8,1024]{2,1,0:T(8,128)(2,1)}), bf16[32,8,1024]{2,1,0:T(8,128)(2,1)S(1)}, u32[]{:S(2)}, u32[]{:S(2)}) async-start(bf16[32,8,1024]{2,1,0:T(8,128)(2,1)} %broadcast_in_dim.68), calls=%async_computation.1 | async-start | bytes 1048576 | tf_op jit(solution)/shard_map/all_to_all | solution.py:27
  46.6 27.2 %copy-start.30 = (s32[512]{0:T(512)}, s32[512]{0:T(512)S(1)}, u32[]{:S(2)}) copy-start(s32[512]{0:T(512)S(1)} %iota_add_fusion) | copy-start | bytes 6148
  63.2 4.2 %copy-start.3 = (bf16[32,8,1024]{2,1,0:T(8,128)(2,1)}, bf16[32,8,1024]{2,1,0:T(8,128)(2,1)S(1)}, u32[]{:S(2)}) copy-start(bf16[32,8,1024]{2,1,0:T(8,128)(2,1)S(1)} %all-to-all-done.1) | copy-start | bytes 1572868
  64.6 18.0 %copy-start.28 = (f32[256]{0:T(256)}, f32[256]{0:T(256)S(1)}, u32[]{:S(2)}) copy-start(f32[256]{0:T(256)S(1)} %get-tuple-element.15) | copy-start | bytes 3076
  65.6 17.0 %copy-start.29 = (f32[256]{0:T(256)}, f32[256]{0:T(256)S(1)}, u32[]{:S(2)}) copy-start(f32[256]{0:T(256)S(1)} %get-tuple-element.17) | copy-start | bytes 3076
  66.7 15.9 %copy-start.26 = (f32[256]{0:T(256)}, f32[256]{0:T(256)S(1)}, u32[]{:S(2)}) copy-start(f32[256]{0:T(256)S(1)} %get-tuple-element.19) | copy-start | bytes 3076
  67.0 15.6 %copy-start.24 = (f32[256]{0:T(256)}, f32[256]{0:T(256)S(1)}, u32[]{:S(2)}) copy-start(f32[256]{0:T(256)S(1)} %get-tuple-element.21) | copy-start | bytes 3076
  67.4 15.2 %copy-start.22 = (f32[256]{0:T(256)}, f32[256]{0:T(256)S(1)}, u32[]{:S(2)}) copy-start(f32[256]{0:T(256)S(1)} %get-tuple-element.23) | copy-start | bytes 3076
  67.7 14.9 %copy-start.20 = (f32[256]{0:T(256)}, f32[256]{0:T(256)S(1)}, u32[]{:S(2)}) copy-start(f32[256]{0:T(256)S(1)} %get-tuple-element.25) | copy-start | bytes 3076
  83.4 15.1 %all-to-all-start.2 = ((f32[32,256,8]{1,2,0:T(8,128)}), f32[32,256,8]{1,2,0:T(8,128)S(1)}, u32[]{:S(2)}, u32[]{:S(2)}) async-start(f32[32,256,8]{1,2,0:T(8,128)} %broadcast_in_dim.79), calls=%async_computation.2 | async-start | bytes 524288 | tf_op jit(solution)/shard_map/all_to_all | solution.py:27
  87.1 4.3 %copy-start.1 = (f32[256,512]{1,0:T(8,128)S(1)}, f32[256,512]{1,0:T(8,128)}, u32[]{:S(2)}) copy-start(f32[256,512]{1,0:T(8,128)} %get-tuple-element.20) | copy-start | bytes 1572868
  87.1 4.3 %copy-start.27 = (f32[256]{0:T(256)S(1)}, f32[256]{0:T(256)}, u32[]{:S(2)}) copy-start(f32[256]{0:T(256)} %copy-done.26) | copy-start | bytes 3076
  87.1 4.2 %copy-start.31 = (s32[512]{0:T(512)S(1)}, s32[512]{0:T(512)}, u32[]{:S(2)}) copy-start(s32[512]{0:T(512)} %copy-done.30) | copy-start | bytes 6148
  87.1 4.2 %copy-start.34 = (s32[256]{0:T(256)S(1)}, s32[256]{0:T(256)}, u32[]{:S(2)}) copy-start(s32[256]{0:T(256)} %param.14) | copy-start | bytes 3076
  87.1 4.2 %copy-start.37 = (bf16[512,128]{1,0:T(8,128)(2,1)S(1)}, bf16[512,128]{1,0:T(8,128)(2,1)}, u32[]{:S(2)}) copy-start(bf16[512,128]{1,0:T(8,128)(2,1)} %param.12) | copy-start | bytes 393220
  89.2 3.2 %copy-start.25 = (f32[256]{0:T(256)S(1)}, f32[256]{0:T(256)}, u32[]{:S(2)}) copy-start(f32[256]{0:T(256)} %copy-done.24) | copy-start | bytes 3076
  91.3 2.1 %copy-start.23 = (f32[256]{0:T(256)S(1)}, f32[256]{0:T(256)}, u32[]{:S(2)}) copy-start(f32[256]{0:T(256)} %copy-done.22) | copy-start | bytes 3076
  92.4 2.2 %copy-start.21 = (f32[256]{0:T(256)S(1)}, f32[256]{0:T(256)}, u32[]{:S(2)}) copy-start(f32[256]{0:T(256)} %copy-done.20) | copy-start | bytes 3076
  93.4 2.2 %copy-start.5 = (f32[32,8,8]{1,0,2:T(8,128)S(1)}, f32[32,8,8]{1,0,2:T(8,128)}, u32[]{:S(2)}) copy-start(f32[32,8,8]{1,0,2:T(8,128)} %constant_dynamic-update-slice_fusion.7) | copy-start | bytes 24580
  93.4 2.2 %copy-start.16 = (f32[32,8,1]{1,0,2:T(8,128)S(1)}, f32[32,8,1]{1,0,2:T(8,128)}, u32[]{:S(2)}) copy-start(f32[32,8,1]{1,0,2:T(8,128)} %stack.58) | copy-start | bytes 3076
  93.4 2.2 %copy-start.17 = (f32[32,8,1]{1,0,2:T(8,128)S(1)}, f32[32,8,1]{1,0,2:T(8,128)}, u32[]{:S(2)}) copy-start(f32[32,8,1]{1,0,2:T(8,128)} %stack.59) | copy-start | bytes 3076
  93.4 2.2 %copy-start.15 = (f32[32,8,1]{1,0,2:T(8,128)S(1)}, f32[32,8,1]{1,0,2:T(8,128)}, u32[]{:S(2)}) copy-start(f32[32,8,1]{1,0,2:T(8,128)} %stack.60) | copy-start | bytes 3076
  93.4 2.2 %copy-start.14 = (f32[32,8,1]{1,0,2:T(8,128)S(1)}, f32[32,8,1]{1,0,2:T(8,128)}, u32[]{:S(2)}) copy-start(f32[32,8,1]{1,0,2:T(8,128)} %stack.61) | copy-start | bytes 3076
  93.4 2.2 %copy-start.13 = (f32[32,8,1]{1,0,2:T(8,128)S(1)}, f32[32,8,1]{1,0,2:T(8,128)}, u32[]{:S(2)}) copy-start(f32[32,8,1]{1,0,2:T(8,128)} %stack.62) | copy-start | bytes 3076
  93.4 2.2 %copy-start.12 = (f32[32,8,1]{1,0,2:T(8,128)S(1)}, f32[32,8,1]{1,0,2:T(8,128)}, u32[]{:S(2)}) copy-start(f32[32,8,1]{1,0,2:T(8,128)} %stack.63) | copy-start | bytes 3076
  93.5 2.2 %copy-start.4 = (f32[32,8,8]{1,0,2:T(8,128)S(1)}, f32[32,8,8]{1,0,2:T(8,128)}, u32[]{:S(2)}) copy-start(f32[32,8,8]{1,0,2:T(8,128)} %constant_dynamic-update-slice_fusion.15) | copy-start | bytes 24580
  93.5 2.2 %copy-start.11 = (f32[32,8,1]{1,0,2:T(8,128)S(1)}, f32[32,8,1]{1,0,2:T(8,128)}, u32[]{:S(2)}) copy-start(f32[32,8,1]{1,0,2:T(8,128)} %stack.67) | copy-start | bytes 3076
  93.5 2.2 %copy-start.10 = (f32[32,8,1]{1,0,2:T(8,128)S(1)}, f32[32,8,1]{1,0,2:T(8,128)}, u32[]{:S(2)}) copy-start(f32[32,8,1]{1,0,2:T(8,128)} %stack.68) | copy-start | bytes 3076
  93.5 2.3 %copy-start.9 = (f32[32,8,1]{1,0,2:T(8,128)S(1)}, f32[32,8,1]{1,0,2:T(8,128)}, u32[]{:S(2)}) copy-start(f32[32,8,1]{1,0,2:T(8,128)} %stack.69) | copy-start | bytes 3076
  93.5 2.3 %copy-start.8 = (f32[32,8,1]{1,0,2:T(8,128)S(1)}, f32[32,8,1]{1,0,2:T(8,128)}, u32[]{:S(2)}) copy-start(f32[32,8,1]{1,0,2:T(8,128)} %stack.70) | copy-start | bytes 3076
  93.5 2.3 %copy-start.7 = (f32[32,8,1]{1,0,2:T(8,128)S(1)}, f32[32,8,1]{1,0,2:T(8,128)}, u32[]{:S(2)}) copy-start(f32[32,8,1]{1,0,2:T(8,128)} %stack.71) | copy-start | bytes 3076
  93.5 2.3 %copy-start.6 = (f32[32,8,1]{1,0,2:T(8,128)S(1)}, f32[32,8,1]{1,0,2:T(8,128)}, u32[]{:S(2)}) copy-start(f32[32,8,1]{1,0,2:T(8,128)} %stack.72) | copy-start | bytes 3076
  93.5 2.3 %copy-start.18 = (f32[32,8,1]{1,0,2:T(8,128)S(1)}, f32[32,8,1]{1,0,2:T(8,128)}, u32[]{:S(2)}) copy-start(f32[32,8,1]{1,0,2:T(8,128)} %stack.73) | copy-start | bytes 3076
  93.5 2.3 %copy-start.19 = (f32[32,8,1]{1,0,2:T(8,128)S(1)}, f32[32,8,1]{1,0,2:T(8,128)}, u32[]{:S(2)}) copy-start(f32[32,8,1]{1,0,2:T(8,128)} %stack.64) | copy-start | bytes 3076
  138.9 20.6 %copy-start.2 = (bf16[1024,256]{1,0:T(8,128)(2,1)S(1)}, bf16[1024,256]{1,0:T(8,128)(2,1)}, u32[]{:S(2)}) copy-start(bf16[1024,256]{1,0:T(8,128)(2,1)} %param.15) | copy-start | bytes 1572868
  160.5 18.2 %all-to-all-start.5 = ((f32[8,32,256]{2,1,0:T(8,128)}), f32[8,32,256]{2,1,0:T(8,128)S(1)}, u32[]{:S(2)}, u32[]{:S(2)}) async-start(f32[8,32,256]{2,1,0:T(8,128)} %fusion.16), calls=%async_computation.5 | async-start | bytes 524288 | tf_op jit(solution)/shard_map/all_to_all | solution.py:15
where the time goes:
time: 181 us; the launch traced here: 180 us
  blocking collectives  58.3 us (32%)
  waiting for transfers between devices  55.2 us (30%)
  starting transfers between devices  25.8 us (14%)
  matrix products  19.1 us (11%)
  local copies, waits for them, and re-layouts  15.1 us (8%)
  other arithmetic  5.98 us (3%)
    all_to_all x1, blocking collectives, summed_on_arrival(): parts = lax.all_to_all(in_blocks(shard, dim, size), axis, 0, 0, tiled=True)  38 us
    all_to_all x2, waiting for transfers between devices, summed_on_arrival(): parts = lax.all_to_all(in_blocks(shard, dim, size), axis, 0, 0, tiled=True)  38 us
    all_to_all x1, blocking collectives, sent_to_all(): return lax.all_to_all(copies, axis, split_axis=0, concat_axis=0, tiled=True)  20.3 us
    all_to_all x2, starting transfers between devices, summed_on_arrival(): parts = lax.all_to_all(in_blocks(shard, dim, size), axis, 0, 0, tiled=True)  18.3 us
    all_to_all x2, waiting for transfers between devices, sent_to_all(): return lax.all_to_all(copies, axis, split_axis=0, concat_axis=0, tiled=True)  17.2 us
    dot_general x8, matrix products, shards(): jnp.dot(weights.astype(jnp.bfloat16), visual_value_cache, preferred_eleme...  10.3 us
    all_to_all x2, starting transfers between devices, sent_to_all(): return lax.all_to_all(copies, axis, split_axis=0, concat_axis=0, tiled=True)  7.55 us
    dot_general x8, matrix products, shards(): lax.dot_general(query_part, visual_key_cache, (((1,), (1,)), ((), ())), p...  5.63 us
  transfers between devices with their start and end apart: 4, of which 4 were waited for; matrix products, arithmetic and copies ran while one was open for 6% of the time, Pallas kernels for 0%

commit v1 on v0

v1 whole, which is shorter than its diff:
```python
import functools

import jax
import jax.numpy as jnp
from jax import lax
from jax.experimental import pallas as pl
from jax.experimental.pallas import tpu as pltpu
from jax.sharding import PartitionSpec as P

MESH = pl.DeviceIdType.MESH
F32, BF16 = jnp.float32, jnp.bfloat16
HEAD = 128
HEADS = 4
WIDE = HEADS * HEAD
SIDE = 128
NEG = -1e30
FLOOR = -1e20
TINY = 1e-30
STEPS = 32000.0
LOG2E = 1.4426950408889634
PLANE = ((2, 3), (2, 2), (1, 3), (3, 3), (1, 2), (3, 2), (0, 3), (0, 2), (2, 1), (1, 1), (3, 1), (2, 0), (0, 1), (1, 0), (3, 0))
OUTER = ((1, 2), (1, 1), (1, 3), (1, 0), (0, 2), (0, 1), (0, 3))


def partner(v, i):
    return (v, v + 1 - 2 * (v % 2), (v + 2) % 4, 3 - v)[i]


def kernel(
    ts_hbm, qw_hbm, gain_hbm, keys, values, seen_hbm, length_hbm, ow_hbm, out,
    gain, seen, length, ts, qw, ow, q_mine, q_other, q_sib, q_part, q_in, q_rows, kb, vb, mark, marks, scores, part, part_in, att, att_sib, o_sum, o_part, o_in,
    swap_s, swap_r, rs1_s, rs1_r, kv_s, kv_r, fw_s, fw_r, ag1_s, ag1_r, rs2_s, rs2_r, ag2_s, ag2_r, c2_s, c2_r, rs3_s, rs3_r, load,
):
    ctx, head, tp = lax.axis_index("ctx"), lax.axis_index("head"), lax.axis_index("tp")
    x, z, c = ctx // 8, (ctx // 2) % 4, ctx % 2
    block = ctx // 2

    def chip(i, j):
        return partner(x, i) * 4 + partner(z, j)

    def on_plane(i, j):
        return (chip(i, j) * 2 + c, head, tp)

    sibling = (block * 2 + 1 - c, head, tp)

    def outer(i, j):
        return (head + i - 2 * i * head) * 4 + partner(tp, j)

    def on_outer(i, j):
        return (ctx, head + i - 2 * i * head, partner(tp, j))

    def copy(src, dst, sems, slot, device):
        return pltpu.make_async_remote_copy(
            src_ref=src, dst_ref=dst, send_sem=sems[0].at[slot], recv_sem=sems[1].at[slot], device_id=device, device_id_type=MESH
        )

    def rows(i, n):
        return pl.ds(pl.multiple_of(i * n, n), n)

    started = []

    def start(cp):
        cp.start()
        started.append(cp)
        return cp

    def arrived(cp):
        cp.wait_recv()

    def loaded(n):
        loads[n].wait()

    mine = pl.ds(pl.multiple_of(c * WIDE, WIDE), WIDE)
    other = pl.ds(pl.multiple_of((1 - c) * WIDE, WIDE), WIDE)
    loads = [
        pltpu.make_async_copy(ts_hbm, ts, load.at[0]),
        pltpu.make_async_copy(qw_hbm, qw, load.at[1]),
        pltpu.make_async_copy(keys, kb.at[0], load.at[2]),
        pltpu.make_async_copy(values, vb.at[0], load.at[3]),
        pltpu.make_async_copy(ow_hbm, ow, load.at[4]),
        pltpu.make_async_copy(gain_hbm, gain, load.at[5]),
        pltpu.make_async_copy(seen_hbm, seen, load.at[6]),
        pltpu.make_async_copy(length_hbm, length, load.at[7]),
    ]
    for cp in loads:
        cp.start()
    barrier = pltpu.get_barrier_semaphore()
    everyone = [on_plane(i, j) for i, j in PLANE] + [sibling] + [on_outer(i, j) for i, j in OUTER]
    for device in everyone:
        pl.semaphore_signal(barrier, inc=1, device_id=device, device_id_type=MESH)

    loaded(6)
    row = lax.broadcasted_iota(jnp.int32, (256, 256), 0)
    col = lax.broadcasted_iota(jnp.int32, (256, 256), 1)
    lane = lax.broadcasted_iota(jnp.int32, (256, SIDE), 1)
    flags = [jnp.sum(jnp.where(row == col, seen[n : n + 1, :].astype(F32), 0.0), axis=1, keepdims=True) for n in (0, 1)]
    mark[...] = jnp.where(lane == 0, flags[0], jnp.where(lane == 1, flags[1], 0.0)).astype(BF16)
    loaded(0)
    loaded(1)
    q_mine[...] = jnp.dot(ts[...], qw[:, mine], preferred_element_type=F32)
    q_other[...] = jnp.dot(ts[...], qw[:, other], preferred_element_type=F32)

    pl.semaphore_wait(barrier, len(everyone))

    halves = {}
    for i in (2, 1, 3, 0):
        part_rows = rows(partner(x, i), 64)
        halves[i] = start(copy(q_other.at[part_rows], q_sib.at[part_rows], (swap_s, swap_r), i, sibling))

    kv = {}

    bufs = ((keys, kb), (values, vb), (mark, marks))

    def of(ref, what, i):
        return ref.at[rows(partner(x, i), 64)] if what == 2 else ref

    def spread(what):
        src, dst = bufs[what]
        for i in (2, 1, 3) if what == 2 else (1, 3):
            kv[what, i] = start(copy(of(src, what, i), dst.at[2 * i], (kv_s, kv_r), 5 * what + i, on_plane(i, 0)))
        kv[what, 0] = start(copy(of(src, what, 0), dst.at[1], (fw_s, fw_r), 4 * what, sibling))

    def pass_on(what, partners):
        for i in partners:
            buf = bufs[what][1]
            for cp in (kv[what, i],) if (what, i) in kv else (kv[what, 4], kv[what, 5]):
                arrived(cp)
            kv[what, -i] = start(copy(buf.at[2 * i], buf.at[2 * i + 1], (fw_s, fw_r), 4 * what + i, sibling))

    def relay(what):
        buf = bufs[what][1]
        for n, i, lo in ((4, 3, 0), (5, 1, 256)):
            piece = pl.ds(lo, 256)
            kv[what, n] = start(copy(buf.at[2 * i, piece], buf.at[4, piece], (kv_s, kv_r), 5 * what + (0 if n == 4 else 4), on_plane(4 - i, 0)))

    spread(0)
    spread(2)

    rs1 = {}
    for i in (2, 1, 3, 0):
        arrived(halves[i])
        part_rows = rows(partner(x, i), 64)
        q = q_mine[part_rows, :] + q_sib[part_rows, :]
        power = jnp.ceil(jnp.log2(jnp.maximum(jnp.max(jnp.abs(q), axis=1, keepdims=True), TINY)))
        q_part[part_rows, :WIDE] = jnp.round(q * (STEPS * jnp.exp2(-power))).astype(jnp.int32).astype(jnp.int16)
        q_part[part_rows, WIDE:] = jnp.broadcast_to(power, (64, SIDE)).astype(jnp.int32).astype(jnp.int16)
        for j in (3, 2, 1, 0):
            if (i, j) != (0, 0):
                src = q_part.at[rows(chip(i, j), 16)]
                rs1[i, j] = start(copy(src, q_in.at[i * 4 + j], (rs1_s, rs1_r), i * 4 + j, on_plane(i, j)))
    spread(1)
    pass_on(0, (1, 3))
    relay(0)
    pass_on(1, (1, 3))
    relay(1)

    def decoded(coded):
        coded = coded.astype(jnp.int32).astype(F32)
        return coded[:, :WIDE] * (jnp.exp2(coded[:, WIDE : WIDE + 1]) / STEPS)

    q_own = decoded(q_part[rows(block, 16), :])
    for i, j in PLANE[::-1]:
        arrived(rs1[i, j])
        q_own = q_own + decoded(q_in[i * 4 + j])
    normed = []
    loaded(5)
    for n in range(HEADS):
        q = q_own[:, n * HEAD : (n + 1) * HEAD]
        mean_sq = jnp.mean(q * q, axis=-1, keepdims=True)
        normed.append((q * lax.rsqrt(mean_sq + 1e-05) * gain[...]).astype(BF16))
    q_rows[rows(z, 16), :] = jnp.concatenate(normed, axis=1)

    ag1 = [start(copy(q_rows.at[rows(z, 16)], q_rows.at[rows(z, 16)], (ag1_s, ag1_r), j, on_plane(0, j))) for j in (3, 2, 1)]

    pass_on(2, (1, 3, 2))
    pass_on(0, (2,))
    pass_on(1, (2,))

    loaded(7)
    row = lax.broadcasted_iota(jnp.int32, (64, 256), 0) + x * 64
    col = lax.broadcasted_iota(jnp.int32, (64, 256), 1)
    reach = jnp.sum(jnp.where(row == col, length[...].astype(F32), 0.0), axis=1, keepdims=True)
    token = lax.broadcasted_iota(jnp.int32, (64, 256), 1)

    for n in (2, 3, 4):
        loaded(n)
    for what in (0, 2):
        for i in (0, -2, -1, -3):
            arrived(kv[what, i])
    for cp in ag1:
        arrived(cp)
    q4 = jnp.concatenate([q_rows[:, n * HEAD : (n + 1) * HEAD] for n in range(HEADS)], axis=0)
    top = jnp.full((4 * 64, 128), NEG, F32)
    for slot in range(8):
        i, d = slot // 2, slot % 2
        k = kb[slot]
        flag = (mark[rows(x, 64), :] if slot == 0 else marks[slot]).astype(F32)
        s = lax.dot_general(q4, k, (((1,), (1,)), ((), ())), preferred_element_type=F32) * (LOG2E / HEAD**0.5)
        first = (chip(i, 0) * 2 + (c if d == 0 else 1 - c)) * 512
        ok = []
        for seg in range(2):
            limit = jnp.where(flag[:, seg : seg + 1] > 0.5, reach, 0.0) - (first + seg * 256).astype(F32)
            ok.append(token.astype(F32) < limit)
        ok = jnp.concatenate([jnp.where(o, 1.0, 0.0) for o in ok], axis=1) > 0.5
        s = jnp.where(ok[None], s.reshape(HEADS, 64, 512), NEG).reshape(HEADS * 64, 512)
        scores[:, slot * 512 : (slot + 1) * 512] = s
        for n in range(4):
            top = jnp.maximum(top, s[:, n * 128 : (n + 1) * 128])
    for i in (0, -2, -1, -3):
        arrived(kv[1, i])
    top = jnp.maximum(jnp.max(top, axis=1, keepdims=True), FLOOR)
    acc = jnp.zeros((HEADS * 64, 2 * HEAD), F32)
    ones = jnp.ones((512, HEAD), BF16)
    for slot in range(8):
        v = vb[slot]
        w = jnp.exp2(scores[:, slot * 512 : (slot + 1) * 512] - top).astype(BF16)
        acc = acc + jnp.dot(w, jnp.concatenate([v, ones], axis=1), preferred_element_type=F32)
    total = acc[:, HEAD:]
    some = total > 0.0
    safe = jnp.where(some, total, 1.0)
    local = acc[:, :HEAD] / safe
    lse = jnp.where(some, top + jnp.log2(safe), NEG)
    lane = lax.broadcasted_iota(jnp.int32, (64, SIDE), 1)
    side = jnp.zeros((64, SIDE), F32)
    for n in range(HEADS):
        part[:, n * HEAD : (n + 1) * HEAD] = local[n * 64 : (n + 1) * 64].astype(BF16)
        side = jnp.where((lane % 8 == n) & (lane < 24), lse[n * 64 : (n + 1) * 64], side)
    hi = side.astype(BF16).astype(F32)
    mid = (side - hi).astype(BF16).astype(F32)
    low = side - hi - mid
    part[:, WIDE:] = jnp.where(lane < 8, hi, jnp.where(lane < 16, mid, low)).astype(BF16)

    rs2 = [start(copy(part.at[rows(partner(z, j), 16)], part_in.at[j], (rs2_s, rs2_r), j, on_plane(0, j))) for j in (3, 2, 1)]
    for cp in rs2:
        arrived(cp)
    pieces = [part[rows(z, 16), :].astype(F32)] + [part_in[j].astype(F32) for j in (1, 2, 3)]
    lses = []
    for p in pieces:
        s = p[:, WIDE:]
        lses.append(s + pltpu.roll(s, SIDE - 8, 1) + pltpu.roll(s, SIDE - 16, 1))
    best = functools.reduce(jnp.maximum, lses)
    shares = [jnp.exp2(s - best) for s in lses]
    norm = functools.reduce(jnp.add, shares)
    shares = [s / norm for s in shares]
    merged = []
    for n in range(HEADS):
        terms = [s[:, n : n + 1] * p[:, n * HEAD : (n + 1) * HEAD] for s, p in zip(shares, pieces)]
        merged.append(functools.reduce(jnp.add, terms).astype(BF16))
    att[rows(block, 16), :] = jnp.concatenate(merged, axis=1)

    ag2 = [start(copy(att.at[rows(block, 16)], att.at[rows(block, 16)], (ag2_s, ag2_r), i * 4 + j, on_plane(i, j))) for i, j in PLANE]
    c2 = [start(copy(att.at[rows(block, 16)], att_sib.at[rows(block, 16)], (c2_s, c2_r), 0, sibling))]
    for cp, (i, j) in reversed(list(zip(ag2, PLANE))):
        arrived(cp)
        piece = rows(chip(i, j), 16)
        c2.append(start(copy(att.at[piece], att_sib.at[piece], (c2_s, c2_r), i * 4 + j, sibling)))
    o_sum[...] = jnp.dot(att[...], ow[mine, :], preferred_element_type=F32)
    for cp in c2:
        arrived(cp)
    o_all = o_sum[...] + jnp.dot(att_sib[...], ow[other, :], preferred_element_type=F32)
    o_sum[...] = o_all
    o_part[...] = o_all.astype(BF16)

    rs3 = [start(copy(o_part.at[rows(outer(i, j), 32)], o_in.at[i * 4 + j], (rs3_s, rs3_r), i * 4 + j, on_outer(i, j))) for i, j in OUTER]
    here = rows(head * 4 + tp, 32)
    result = ts[here, :].astype(F32) + o_sum[here, :]
    for cp, (i, j) in zip(rs3, OUTER):
        arrived(cp)
        result = result + o_in[i * 4 + j].astype(F32)
    out[...] = result.astype(BF16)
    for cp in started:
        cp.wait_send()


def shards(text_states, q_weight, q_gain, visual_key_cache, visual_value_cache, block_mask, lengths, o_weight):
    vmem = pl.BlockSpec(memory_space=pltpu.VMEM)
    hbm = pl.BlockSpec(memory_space=pltpu.HBM)
    dma = pltpu.SemaphoreType.DMA
    return pl.pallas_call(
        kernel,
        out_shape=jax.ShapeDtypeStruct((32, 256), BF16),
        in_specs=[hbm] * 8,
        out_specs=vmem,
        scratch_shapes=[
            pltpu.VMEM((1, HEAD), F32),
            pltpu.VMEM((2, 256), jnp.int32),
            pltpu.VMEM((1, 256), jnp.int32),
            pltpu.VMEM((256, 256), BF16),
            pltpu.VMEM((256, 2 * WIDE), BF16),
            pltpu.VMEM((2 * WIDE, 256), BF16),
            pltpu.VMEM((256, WIDE), F32),
            pltpu.VMEM((256, WIDE), F32),
            pltpu.VMEM((256, WIDE), F32),
            pltpu.VMEM((256, WIDE + SIDE), jnp.int16),
            pltpu.VMEM((16, 16, WIDE + SIDE), jnp.int16),
            pltpu.VMEM((64, WIDE), BF16),
            pltpu.VMEM((8, 512, HEAD), BF16),
            pltpu.VMEM((8, 512, HEAD), BF16),
            pltpu.VMEM((256, SIDE), BF16),
            pltpu.VMEM((8, 64, SIDE), BF16),
            pltpu.VMEM((HEADS * 64, 4096), F32),
            pltpu.VMEM((64, WIDE + SIDE), BF16),
            pltpu.VMEM((4, 16, WIDE + SIDE), BF16),
            pltpu.VMEM((256, WIDE), BF16),
            pltpu.VMEM((256, WIDE), BF16),
            pltpu.VMEM((256, 256), F32),
            pltpu.VMEM((256, 256), BF16),
            pltpu.VMEM((8, 32, 256), BF16),
            dma((4,)), dma((4,)),
            dma((16,)), dma((16,)),
            dma((15,)), dma((15,)),
            dma((12,)), dma((12,)),
            dma((4,)), dma((4,)),
            dma((4,)), dma((4,)),
            dma((16,)), dma((16,)),
            dma((16,)), dma((16,)),
            dma((8,)), dma((8,)),
            dma((8,)),
        ],
        compiler_params=pltpu.CompilerParams(collective_id=0, has_side_effects=True, vmem_limit_bytes=60 * 1024 * 1024),
    )(text_states, q_weight, q_gain.reshape(1, HEAD), visual_key_cache, visual_value_cache, block_mask.T, lengths.reshape(1, 256), o_weight)


def solution(mesh):
    in_specs = (
        P(None, "ctx"),
        P("ctx", ("head", "tp")),
        P(),
        P("ctx", ("head", "tp")),
        P("ctx", ("head", "tp")),
        P(None, "ctx"),
        P(),
        P(("head", "tp"), "ctx"),
    )
    out_specs = P(("head", "tp"), "ctx")
    return jax.shard_map(shards, mesh=mesh, in_specs=in_specs, out_specs=out_specs, check_vma=False)
```

time: 181 us -> 52.5 us (0.29)
  blocking collectives: 58.3 us -> 0 us
  waiting for transfers between devices: 55.2 us -> 0 us
  Pallas kernels: 0 us -> 51 us
  starting transfers between devices: 25.8 us -> 0 us
  matrix products: 19.1 us -> 0 us
  local copies, waits for them, and re-layouts: 15.1 us -> 1.32 us
  other arithmetic: 5.98 us -> 0 us
    all_to_all x2 -> x0, blocking collectives: 58.3 us -> none  [the longest x1 38 us: summed_on_arrival(): parts = lax.all_to_all(in_blocks(shard, dim, size), axis, 0, 0, tiled=True)]
    all_to_all x4 -> x0, waiting for transfers between devices: 55.2 us -> none  [the longest x2 38 us: summed_on_arrival(): parts = lax.all_to_all(in_blocks(shard, dim, size), axis, 0, 0, tiled=True)]
    pallas_call x0 -> x1, Pallas kernels: none -> 51 us  [shards(): pl.pallas_call(kernel, out_shape=jax.ShapeDtypeStruct((32, 256), BF16), i...]
    all_to_all x4 -> x0, starting transfers between devices: 25.8 us -> none  [the longest x2 18.3 us: summed_on_arrival(): parts = lax.all_to_all(in_blocks(shard, dim, size), axis, 0, 0, tiled=True)]
    dot_general x18 -> x0, matrix products: 19.1 us -> none  [the longest x8 10.3 us: shards(): jnp.dot(weights.astype(jnp.bfloat16), visual_value_cache, preferred_eleme...]
    another operation x18 -> x0, local copies, waits for them, and re-layouts: 9.82 us -> none  [the longest x9 4.93 us: shards(): local_max = jnp.stack(partial_maxes, axis=1)]
    reduce_sum x5 -> x0, other arithmetic: 2.94 us -> none  [the longest x1 2.7 us: shards(): partial_totals.append(jnp.sum(weights, axis=1))]
    broadcast_in_dim x5 -> x0, local copies, waits for them, and re-layouts: 2.01 us -> none  [the longest x3 1.64 us: sent_to_all(): copies = jnp.broadcast_to(shard, (lax.axis_size(axis), *shard.shape))]
  transfers between devices with their start and end apart: 4 -> 0, of which waited for: 4 -> 0; matrix products, arithmetic and copies ran while one was open for 6% -> 0% of each run, Pallas kernels for 0% -> 0%
where the time goes in v1:
time: 52.5 us; the launch traced here: 52.4 us
  Pallas kernels  51 us (97%)
  local copies, waits for them, and re-layouts  1.32 us (3%)
    pallas_call x1, Pallas kernels, shards(): pl.pallas_call(kernel, out_shape=jax.ShapeDtypeStruct((32, 256), BF16), i...  51 us
    unnamed x1, local copies, waits for them, and re-layouts  1.32 us

profile of v1, /device:TPU:1, one launch (start us, length us, event | category | flops | bytes accessed | tf_op | source)
XLA Modules:
  0.0 52.4 jit_solution(11220803192038855526)
XLA Ops:
  0.0 51.0 %shard_map.82 = bf16[32,256]{1,0:T(8,128)(2,1)} custom-call(bf16[256,256]{1,0:T(8,128)(2,1)} %ts_hbm.1, bf16[256,1024]{1,0:T(8,128)(2,1)} %qw_hbm.1, f32[1,128]{1,0:T(1,128)} %bitcast.5, bf16[512,128]{1,0:T(8,128)(2,1)} %keys.1, bf16[512,128]{1,0:T(8,128)(2,1)} %values.1, s32[2,256]{1,0:T(2,128)} %bitcast.3, s32[1,256]{1,0:T(1,128)} %bitcast.4, ...), custom_call_target="tpu_custom_call" | custom-call | tf_op jit(solution)/shard_map/pallas_call | solution.py:279
  51.0 1.3 %copy.10 = bf16[32,256]{1,0:T(8,128)(2,1)} copy(bf16[32,256]{1,0:T(8,128)(2,1)} %shard_map.82) | data formatting | bytes 32768

commit v2 on v1

--- a/solution.py
+++ b/solution.py
@@ -28,7 +28,7 @@
 
 def kernel(
     ts_hbm, qw_hbm, gain_hbm, keys, values, seen_hbm, length_hbm, ow_hbm, out,
-    gain, seen, length, ts, qw, ow, q_mine, q_other, q_sib, q_part, q_in, q_rows, kb, vb, mark, marks, scores, part, part_in, att, att_sib, o_sum, o_part, o_in,
+    gain, seen, length, ts, qw, ow, q_mine, q_other, q_sib, q_part, q_pow, q_in, pow_in, q_rows, kb, vb, mark, marks, scores, part, part_in, att, att_sib, o_sum, o_part, o_in,
     swap_s, swap_r, rs1_s, rs1_r, kv_s, kv_r, fw_s, fw_r, ag1_s, ag1_r, rs2_s, rs2_r, ag2_s, ag2_r, c2_s, c2_r, rs3_s, rs3_r, load,
 ):
     ctx, head, tp = lax.axis_index("ctx"), lax.axis_index("head"), lax.axis_index("tp")
@@ -136,32 +136,39 @@
     spread(0)
     spread(2)
 
+    diagonal = lax.broadcasted_iota(jnp.int32, (16, 128), 0) == lax.broadcasted_iota(jnp.int32, (16, 128), 1)
+
     rs1 = {}
     for i in (2, 1, 3, 0):
         arrived(halves[i])
         part_rows = rows(partner(x, i), 64)
         q = q_mine[part_rows, :] + q_sib[part_rows, :]
         power = jnp.ceil(jnp.log2(jnp.maximum(jnp.max(jnp.abs(q), axis=1, keepdims=True), TINY)))
-        q_part[part_rows, :WIDE] = jnp.round(q * (STEPS * jnp.exp2(-power))).astype(jnp.int32).astype(jnp.int16)
-        q_part[part_rows, WIDE:] = jnp.broadcast_to(power, (64, SIDE)).astype(jnp.int32).astype(jnp.int16)
+        q_part[part_rows, :] = jnp.round(q * (STEPS * jnp.exp2(-power))).astype(jnp.int32).astype(jnp.int16)
+        for n in range(4):
+            laid = jnp.where(diagonal, power[16 * n : 16 * n + 16], 0.0)
+            q_pow[partner(x, i) * 4 + n] = jnp.sum(laid, axis=0, keepdims=True)
         for j in (3, 2, 1, 0):
             if (i, j) != (0, 0):
                 src = q_part.at[rows(chip(i, j), 16)]
                 rs1[i, j] = start(copy(src, q_in.at[i * 4 + j], (rs1_s, rs1_r), i * 4 + j, on_plane(i, j)))
+                src = q_pow.at[chip(i, j)]
+                rs1[j, i, 1] = start(copy(src, pow_in.at[i * 4 + j], (rs1_s, rs1_r), 16 + i * 4 + j, on_plane(i, j)))
     spread(1)
     pass_on(0, (1, 3))
     relay(0)
     pass_on(1, (1, 3))
     relay(1)
 
-    def decoded(coded):
-        coded = coded.astype(jnp.int32).astype(F32)
-        return coded[:, :WIDE] * (jnp.exp2(coded[:, WIDE : WIDE + 1]) / STEPS)
-
-    q_own = decoded(q_part[rows(block, 16), :])
+    def decoded(coded, powers):
+        power = jnp.sum(jnp.where(diagonal, powers, 0.0), axis=1, keepdims=True)
+        return coded.astype(jnp.int32).astype(F32) * (jnp.exp2(power) / STEPS)
+
+    q_own = decoded(q_part[rows(block, 16), :], q_pow[block])
     for i, j in PLANE[::-1]:
         arrived(rs1[i, j])
-        q_own = q_own + decoded(q_in[i * 4 + j])
+        arrived(rs1[j, i, 1])
+        q_own = q_own + decoded(q_in[i * 4 + j], pow_in[i * 4 + j])
     normed = []
     loaded(5)
     for n in range(HEADS):
@@ -209,63 +216,77 @@
     for i in (0, -2, -1, -3):
         arrived(kv[1, i])
     top = jnp.maximum(jnp.max(top, axis=1, keepdims=True), FLOOR)
-    acc = jnp.zeros((HEADS * 64, 2 * HEAD), F32)
     ones = jnp.ones((512, HEAD), BF16)
-    for slot in range(8):
-        v = vb[slot]
-        w = jnp.exp2(scores[:, slot * 512 : (slot + 1) * 512] - top).astype(BF16)
-        acc = acc + jnp.dot(w, jnp.concatenate([v, ones], axis=1), preferred_element_type=F32)
-    total = acc[:, HEAD:]
-    some = total > 0.0
-    safe = jnp.where(some, total, 1.0)
-    local = acc[:, :HEAD] / safe
-    lse = jnp.where(some, top + jnp.log2(safe), NEG)
     lane = lax.broadcasted_iota(jnp.int32, (64, SIDE), 1)
-    side = jnp.zeros((64, SIDE), F32)
-    for n in range(HEADS):
-        part[:, n * HEAD : (n + 1) * HEAD] = local[n * 64 : (n + 1) * 64].astype(BF16)
-        side = jnp.where((lane % 8 == n) & (lane < 24), lse[n * 64 : (n + 1) * 64], side)
-    hi = side.astype(BF16).astype(F32)
-    mid = (side - hi).astype(BF16).astype(F32)
-    low = side - hi - mid
-    part[:, WIDE:] = jnp.where(lane < 8, hi, jnp.where(lane < 16, mid, low)).astype(BF16)
-
-    rs2 = [start(copy(part.at[rows(partner(z, j), 16)], part_in.at[j], (rs2_s, rs2_r), j, on_plane(0, j))) for j in (3, 2, 1)]
-    for cp in rs2:
-        arrived(cp)
-    pieces = [part[rows(z, 16), :].astype(F32)] + [part_in[j].astype(F32) for j in (1, 2, 3)]
-    lses = []
-    for p in pieces:
-        s = p[:, WIDE:]
-        lses.append(s + pltpu.roll(s, SIDE - 8, 1) + pltpu.roll(s, SIDE - 16, 1))
-    best = functools.reduce(jnp.maximum, lses)
-    shares = [jnp.exp2(s - best) for s in lses]
-    norm = functools.reduce(jnp.add, shares)
-    shares = [s / norm for s in shares]
-    merged = []
-    for n in range(HEADS):
-        terms = [s[:, n : n + 1] * p[:, n * HEAD : (n + 1) * HEAD] for s, p in zip(shares, pieces)]
-        merged.append(functools.reduce(jnp.add, terms).astype(BF16))
-    att[rows(block, 16), :] = jnp.concatenate(merged, axis=1)
-
-    ag2 = [start(copy(att.at[rows(block, 16)], att.at[rows(block, 16)], (ag2_s, ag2_r), i * 4 + j, on_plane(i, j))) for i, j in PLANE]
-    c2 = [start(copy(att.at[rows(block, 16)], att_sib.at[rows(block, 16)], (c2_s, c2_r), 0, sibling))]
-    for cp, (i, j) in reversed(list(zip(ag2, PLANE))):
-        arrived(cp)
-        piece = rows(chip(i, j), 16)
-        c2.append(start(copy(att.at[piece], att_sib.at[piece], (c2_s, c2_r), i * 4 + j, sibling)))
-    o_sum[...] = jnp.dot(att[...], ow[mine, :], preferred_element_type=F32)
-    for cp in c2:
-        arrived(cp)
-    o_all = o_sum[...] + jnp.dot(att_sib[...], ow[other, :], preferred_element_type=F32)
+    rs2 = {}
+    for g in range(2):
+        mid_rows = slice(g * 128, (g + 1) * 128)
+        acc = jnp.zeros((128, 2 * HEAD), F32)
+        for slot in range(8):
+            w = jnp.exp2(scores[mid_rows, slot * 512 : (slot + 1) * 512] - top[mid_rows]).astype(BF16)
+            acc = acc + jnp.dot(w, jnp.concatenate([vb[slot], ones], axis=1), preferred_element_type=F32)
+        total = acc[:, HEAD:]
+        some = total > 0.0
+        safe = jnp.where(some, total, 1.0)
+        local = acc[:, :HEAD] / safe
+        lse = jnp.where(some, top[mid_rows] + jnp.log2(safe), NEG)
+        side = jnp.zeros((64, SIDE), F32)
+        for n in range(2):
+            part[g, :, n * HEAD : (n + 1) * HEAD] = local[n * 64 : (n + 1) * 64].astype(BF16)
+            side = jnp.where((lane % 8 == n) & (lane < 24), lse[n * 64 : (n + 1) * 64], side)
+        hi = side.astype(BF16).astype(F32)
+        mid = (side - hi).astype(BF16).astype(F32)
+        low = side - hi - mid
+        part[g, :, 2 * HEAD :] = jnp.where(lane < 8, hi, jnp.where(lane < 16, mid, low)).astype(BF16)
+        for j in (3, 2, 1):
+            src = part.at[g, rows(partner(z, j), 16)]
+            rs2[g, j] = start(copy(src, part_in.at[g, j], (rs2_s, rs2_r), 4 * g + j, on_plane(0, j)))
+
+    ag2 = {}
+    for g in range(2):
+        for j in (1, 2, 3):
+            arrived(rs2[g, j])
+        pieces = [part[g, rows(z, 16), :].astype(F32)] + [part_in[g, j].astype(F32) for j in (1, 2, 3)]
+        lses = []
+        for p in pieces:
+            s = p[:, 2 * HEAD :]
+            lses.append(s + pltpu.roll(s, SIDE - 8, 1) + pltpu.roll(s, SIDE - 16, 1))
+        best = functools.reduce(jnp.maximum, lses)
+        shares = [jnp.exp2(s - best) for s in lses]
+        norm = functools.reduce(jnp.add, shares)
+        shares = [s / norm for s in shares]
+        merged = []
+        for n in range(2):
+            terms = [s[:, n : n + 1] * p[:, n * HEAD : (n + 1) * HEAD] for s, p in zip(shares, pieces)]
+            merged.append(functools.reduce(jnp.add, terms).astype(BF16))
+        att[g, rows(block, 16), :] = jnp.concatenate(merged, axis=1)
+        for i, j in PLANE:
+            piece = att.at[g, rows(block, 16)]
+            ag2[g, i, j] = start(copy(piece, piece, (ag2_s, ag2_r), 16 * g + i * 4 + j, on_plane(i, j)))
+
+    def weights(core, g):
+        return ow[pl.ds(pl.multiple_of(core * WIDE + g * 256, 256), 256), :]
+
+    c2 = []
+    for g in range(2):
+        for i, j in PLANE[::-1]:
+            arrived(ag2[g, i, j])
+        c2.append(start(copy(att.at[g], att_sib.at[g], (c2_s, c2_r), g, sibling)))
+        if g == 0:
+            o_sum[...] = jnp.dot(att[0], weights(c, 0), preferred_element_type=F32)
+    arrived(c2[0])
+    o_sum[...] += jnp.dot(att[1], weights(c, 1), preferred_element_type=F32) + jnp.dot(att_sib[0], weights(1 - c, 0), preferred_element_type=F32)
+    arrived(c2[1])
+    o_all = o_sum[...] + jnp.dot(att_sib[1], weights(1 - c, 1), preferred_element_type=F32)
     o_sum[...] = o_all
     o_part[...] = o_all.astype(BF16)
-
-    rs3 = [start(copy(o_part.at[rows(outer(i, j), 32)], o_in.at[i * 4 + j], (rs3_s, rs3_r), i * 4 + j, on_outer(i, j))) for i, j in OUTER]
+    rs3 = {}
+    for i, j in OUTER:
+        rs3[i, j] = start(copy(o_part.at[rows(outer(i, j), 32)], o_in.at[i * 4 + j], (rs3_s, rs3_r), i * 4 + j, on_outer(i, j)))
     here = rows(head * 4 + tp, 32)
     result = ts[here, :].astype(F32) + o_sum[here, :]
-    for cp, (i, j) in zip(rs3, OUTER):
-        arrived(cp)
+    for i, j in OUTER[::-1]:
+        arrived(rs3[i, j])
         result = result + o_in[i * 4 + j].astype(F32)
     out[...] = result.astype(BF16)
     for cp in started:
@@ -291,34 +312,36 @@
             pltpu.VMEM((256, WIDE), F32),
             pltpu.VMEM((256, WIDE), F32),
             pltpu.VMEM((256, WIDE), F32),
-            pltpu.VMEM((256, WIDE + SIDE), jnp.int16),
-            pltpu.VMEM((16, 16, WIDE + SIDE), jnp.int16),
+            pltpu.VMEM((256, WIDE), jnp.int16),
+            pltpu.VMEM((16, 1, 128), F32),
+            pltpu.VMEM((16, 16, WIDE), jnp.int16),
+            pltpu.VMEM((16, 1, 128), F32),
             pltpu.VMEM((64, WIDE), BF16),
             pltpu.VMEM((8, 512, HEAD), BF16),
             pltpu.VMEM((8, 512, HEAD), BF16),
             pltpu.VMEM((256, SIDE), BF16),
             pltpu.VMEM((8, 64, SIDE), BF16),
             pltpu.VMEM((HEADS * 64, 4096), F32),
-            pltpu.VMEM((64, WIDE + SIDE), BF16),
-            pltpu.VMEM((4, 16, WIDE + SIDE), BF16),
-            pltpu.VMEM((256, WIDE), BF16),
-            pltpu.VMEM((256, WIDE), BF16),
+            pltpu.VMEM((2, 64, 2 * HEAD + SIDE), BF16),
+            pltpu.VMEM((2, 4, 16, 2 * HEAD + SIDE), BF16),
+            pltpu.VMEM((2, 256, 2 * HEAD), BF16),
+            pltpu.VMEM((2, 256, 2 * HEAD), BF16),
             pltpu.VMEM((256, 256), F32),
             pltpu.VMEM((256, 256), BF16),
             pltpu.VMEM((8, 32, 256), BF16),
             dma((4,)), dma((4,)),
-            dma((16,)), dma((16,)),
+            dma((32,)), dma((32,)),
             dma((15,)), dma((15,)),
             dma((12,)), dma((12,)),
             dma((4,)), dma((4,)),
-            dma((4,)), dma((4,)),
-            dma((16,)), dma((16,)),
-            dma((16,)), dma((16,)),
+            dma((8,)), dma((8,)),
+            dma((32,)), dma((32,)),
+            dma((2,)), dma((2,)),
             dma((8,)), dma((8,)),
             dma((8,)),
         ],
-        compiler_params=pltpu.CompilerParams(collective_id=0, has_side_effects=True, vmem_limit_bytes=60 * 1024 * 1024),
-    )(text_states, q_weight, q_gain.reshape(1, HEAD), visual_key_cache, visual_value_cache, block_mask.T, lengths.reshape(1, 256), o_weight)
+        compiler_params=pltpu.CompilerParams(collective_id=0, has_side_effects=True, vmem_limit_bytes=40 * 1024 * 1024),
+    )(*[pltpu.with_memory_space_constraint(a, pltpu.HBM) for a in (text_states, q_weight, q_gain.reshape(1, HEAD), visual_key_cache, visual_value_cache, block_mask.T, lengths.reshape(1, 256), o_weight)])
 
 
 def solution(mesh):

time: 52.5 us -> 50.8 us (0.968)
  Pallas kernels: 51 us -> 50.1 us
  local copies, waits for them, and re-layouts: 1.32 us -> 0.61 us
    pallas_call x1, Pallas kernels: 51 us -> 50.1 us  [shards(): pl.pallas_call(kernel, out_shape=jax.ShapeDtypeStruct((32, 256), BF16), i...]
    unnamed x1, local copies, waits for them, and re-layouts: 1.32 us -> 0.61 us
where the time goes in v2:
time: 50.8 us; the launch traced here: 50.7 us
  Pallas kernels  50.1 us (99%)
  local copies, waits for them, and re-layouts  0.61 us (1%)
    pallas_call x1, Pallas kernels, shards(): pl.pallas_call(kernel, out_shape=jax.ShapeDtypeStruct((32, 256), BF16), i...  50.1 us

profile of v2, /device:TPU:1, one launch (start us, length us, event | category | flops | bytes accessed | tf_op | source)
XLA Modules:
  0.0 50.7 jit_solution(17630238584670871733)
XLA Ops:
  0.0 50.1 %shard_map.82 = bf16[32,256]{1,0:T(8,128)(2,1)S(1)} custom-call(bf16[256,256]{1,0:T(8,128)(2,1)} %ts_hbm.1, bf16[256,1024]{1,0:T(8,128)(2,1)} %qw_hbm.1, f32[1,128]{1,0:T(1,128)} %bitcast.5, bf16[512,128]{1,0:T(8,128)(2,1)} %keys.1, bf16[512,128]{1,0:T(8,128)(2,1)} %values.1, s32[2,256]{1,0:T(2,128)} %bitcast.3, s32[1,256]{1,0:T(1,128)} %bitcast.4, ...), custom_call_target="tpu_custom_call" | custom-call | tf_op jit(solution)/shard_map/pallas_call | solution.py:300
  50.1 0.6 %copy.10 = bf16[32,256]{1,0:T(8,128)(2,1)} copy(bf16[32,256]{1,0:T(8,128)(2,1)S(1)} %shard_map.82) | data formatting | bytes 32768

commit v3 on v2

--- a/solution.py
+++ b/solution.py
@@ -69,6 +69,11 @@
 
     def loaded(n):
         loads[n].wait()
+
+    barrier = pltpu.get_barrier_semaphore()
+    everyone = [on_outer(i, j) for i, j in OUTER] + [on_plane(i, j) for i, j in PLANE] + [sibling]
+    for device in everyone:
+        pl.semaphore_signal(barrier, inc=1, device_id=device, device_id_type=MESH)
 
     mine = pl.ds(pl.multiple_of(c * WIDE, WIDE), WIDE)
     other = pl.ds(pl.multiple_of((1 - c) * WIDE, WIDE), WIDE)
@@ -84,11 +89,6 @@
     ]
     for cp in loads:
         cp.start()
-    barrier = pltpu.get_barrier_semaphore()
-    everyone = [on_plane(i, j) for i, j in PLANE] + [sibling] + [on_outer(i, j) for i, j in OUTER]
-    for device in everyone:
-        pl.semaphore_signal(barrier, inc=1, device_id=device, device_id_type=MESH)
-
     loaded(6)
     row = lax.broadcasted_iota(jnp.int32, (256, 256), 0)
     col = lax.broadcasted_iota(jnp.int32, (256, 256), 1)
@@ -103,7 +103,7 @@
     pl.semaphore_wait(barrier, len(everyone))
 
     halves = {}
-    for i in (2, 1, 3, 0):
+    for i in (0, 2, 1, 3):
         part_rows = rows(partner(x, i), 64)
         halves[i] = start(copy(q_other.at[part_rows], q_sib.at[part_rows], (swap_s, swap_r), i, sibling))
 
@@ -139,7 +139,7 @@
     diagonal = lax.broadcasted_iota(jnp.int32, (16, 128), 0) == lax.broadcasted_iota(jnp.int32, (16, 128), 1)
 
     rs1 = {}
-    for i in (2, 1, 3, 0):
+    for i in (0, 2, 1, 3):
         arrived(halves[i])
         part_rows = rows(partner(x, i), 64)
         q = q_mine[part_rows, :] + q_sib[part_rows, :]
@@ -157,8 +157,6 @@
     spread(1)
     pass_on(0, (1, 3))
     relay(0)
-    pass_on(1, (1, 3))
-    relay(1)
 
     def decoded(coded, powers):
         power = jnp.sum(jnp.where(diagonal, powers, 0.0), axis=1, keepdims=True)
@@ -179,9 +177,10 @@
 
     ag1 = [start(copy(q_rows.at[rows(z, 16)], q_rows.at[rows(z, 16)], (ag1_s, ag1_r), j, on_plane(0, j))) for j in (3, 2, 1)]
 
+    pass_on(1, (1, 3))
+    relay(1)
     pass_on(2, (1, 3, 2))
     pass_on(0, (2,))
-    pass_on(1, (2,))
 
     loaded(7)
     row = lax.broadcasted_iota(jnp.int32, (64, 256), 0) + x * 64
@@ -196,6 +195,7 @@
             arrived(kv[what, i])
     for cp in ag1:
         arrived(cp)
+    token_f = token.astype(F32)
     q4 = jnp.concatenate([q_rows[:, n * HEAD : (n + 1) * HEAD] for n in range(HEADS)], axis=0)
     top = jnp.full((4 * 64, 128), NEG, F32)
     for slot in range(8):
@@ -204,16 +204,14 @@
         flag = (mark[rows(x, 64), :] if slot == 0 else marks[slot]).astype(F32)
         s = lax.dot_general(q4, k, (((1,), (1,)), ((), ())), preferred_element_type=F32) * (LOG2E / HEAD**0.5)
         first = (chip(i, 0) * 2 + (c if d == 0 else 1 - c)) * 512
-        ok = []
         for seg in range(2):
             limit = jnp.where(flag[:, seg : seg + 1] > 0.5, reach, 0.0) - (first + seg * 256).astype(F32)
-            ok.append(token.astype(F32) < limit)
-        ok = jnp.concatenate([jnp.where(o, 1.0, 0.0) for o in ok], axis=1) > 0.5
-        s = jnp.where(ok[None], s.reshape(HEADS, 64, 512), NEG).reshape(HEADS * 64, 512)
-        scores[:, slot * 512 : (slot + 1) * 512] = s
-        for n in range(4):
-            top = jnp.maximum(top, s[:, n * 128 : (n + 1) * 128])
-    for i in (0, -2, -1, -3):
+            ok = token_f < limit
+            allowed = jnp.where(ok[None], s[:, seg * 256 : (seg + 1) * 256].reshape(HEADS, 64, 256), NEG).reshape(HEADS * 64, 256)
+            scores[:, slot * 512 + seg * 256 : slot * 512 + (seg + 1) * 256] = allowed
+            top = jnp.maximum(top, jnp.maximum(allowed[:, :128], allowed[:, 128:]))
+    pass_on(1, (2,))
+    for i in (0, -1, -3):
         arrived(kv[1, i])
     top = jnp.maximum(jnp.max(top, axis=1, keepdims=True), FLOOR)
     ones = jnp.ones((512, HEAD), BF16)
@@ -222,7 +220,9 @@
     for g in range(2):
         mid_rows = slice(g * 128, (g + 1) * 128)
         acc = jnp.zeros((128, 2 * HEAD), F32)
-        for slot in range(8):
+        for slot in (0, 1, 2, 6, 3, 7, 5, 4):
+            if g == 0 and slot == 5:
+                arrived(kv[1, -2])
             w = jnp.exp2(scores[mid_rows, slot * 512 : (slot + 1) * 512] - top[mid_rows]).astype(BF16)
             acc = acc + jnp.dot(w, jnp.concatenate([vb[slot], ones], axis=1), preferred_element_type=F32)
         total = acc[:, HEAD:]

time: 50.8 us -> 50 us (0.984)
  Pallas kernels: 50.1 us -> 49.3 us
    pallas_call x1, Pallas kernels: 50.1 us -> 49.3 us  [shards(): pl.pallas_call(kernel, out_shape=jax.ShapeDtypeStruct((32, 256), BF16), i...]
where the time goes in v3:
time: 50 us; the launch traced here: 49.9 us
  Pallas kernels  49.3 us (99%)
  local copies, waits for them, and re-layouts  0.61 us (1%)
    pallas_call x1, Pallas kernels, shards(): pl.pallas_call(kernel, out_shape=jax.ShapeDtypeStruct((32, 256), BF16), i...  49.3 us

profile of v3, /device:TPU:1, one launch (start us, length us, event | category | flops | bytes accessed | tf_op | source)
XLA Modules:
  0.0 49.9 jit_solution(11828562895552113305)
XLA Ops:
  0.0 49.3 %shard_map.82 = bf16[32,256]{1,0:T(8,128)(2,1)S(1)} custom-call(bf16[256,256]{1,0:T(8,128)(2,1)} %ts_hbm.1, bf16[256,1024]{1,0:T(8,128)(2,1)} %qw_hbm.1, f32[1,128]{1,0:T(1,128)} %bitcast.5, bf16[512,128]{1,0:T(8,128)(2,1)} %keys.1, bf16[512,128]{1,0:T(8,128)(2,1)} %values.1, s32[2,256]{1,0:T(2,128)} %bitcast.3, s32[1,256]{1,0:T(1,128)} %bitcast.4, ...), custom_call_target="tpu_custom_call" | custom-call | tf_op jit(solution)/shard_map/pallas_call | solution.py:300
  49.3 0.6 %copy.10 = bf16[32,256]{1,0:T(8,128)(2,1)} copy(bf16[32,256]{1,0:T(8,128)(2,1)S(1)} %shard_map.82) | data formatting | bytes 32768

commit v4 on v3

--- a/solution.py
+++ b/solution.py
@@ -134,7 +134,6 @@
             kv[what, n] = start(copy(buf.at[2 * i, piece], buf.at[4, piece], (kv_s, kv_r), 5 * what + (0 if n == 4 else 4), on_plane(4 - i, 0)))
 
     spread(0)
-    spread(2)
 
     diagonal = lax.broadcasted_iota(jnp.int32, (16, 128), 0) == lax.broadcasted_iota(jnp.int32, (16, 128), 1)
 
@@ -155,6 +154,7 @@
                 src = q_pow.at[chip(i, j)]
                 rs1[j, i, 1] = start(copy(src, pow_in.at[i * 4 + j], (rs1_s, rs1_r), 16 + i * 4 + j, on_plane(i, j)))
     spread(1)
+    spread(2)
     pass_on(0, (1, 3))
     relay(0)
 

time: 50 us -> 49.3 us (0.986)
  Pallas kernels: 49.3 us -> 48.6 us
    pallas_call x1, Pallas kernels: 49.3 us -> 48.6 us  [shards(): pl.pallas_call(kernel, out_shape=jax.ShapeDtypeStruct((32, 256), BF16), i...]
where the time goes in v4:
time: 49.3 us; the launch traced here: 49.2 us
  Pallas kernels  48.6 us (99%)
  local copies, waits for them, and re-layouts  0.61 us (1%)
    pallas_call x1, Pallas kernels, shards(): pl.pallas_call(kernel, out_shape=jax.ShapeDtypeStruct((32, 256), BF16), i...  48.6 us

profile of v4, /device:TPU:1, one launch (start us, length us, event | category | flops | bytes accessed | tf_op | source)
XLA Modules:
  0.0 49.2 jit_solution(16392886775630677070)
XLA Ops:
  0.0 48.6 %shard_map.82 = bf16[32,256]{1,0:T(8,128)(2,1)S(1)} custom-call(bf16[256,256]{1,0:T(8,128)(2,1)} %ts_hbm.1, bf16[256,1024]{1,0:T(8,128)(2,1)} %qw_hbm.1, f32[1,128]{1,0:T(1,128)} %bitcast.5, bf16[512,128]{1,0:T(8,128)(2,1)} %keys.1, bf16[512,128]{1,0:T(8,128)(2,1)} %values.1, s32[2,256]{1,0:T(2,128)} %bitcast.3, s32[1,256]{1,0:T(1,128)} %bitcast.4, ...), custom_call_target="tpu_custom_call" | custom-call | tf_op jit(solution)/shard_map/pallas_call | solution.py:300
  48.6 0.6 %copy.10 = bf16[32,256]{1,0:T(8,128)(2,1)} copy(bf16[32,256]{1,0:T(8,128)(2,1)S(1)} %shard_map.82) | data formatting | bytes 32768

commit v5 on v4

--- a/solution.py
+++ b/solution.py
@@ -117,8 +117,8 @@
     def spread(what):
         src, dst = bufs[what]
         for i in (2, 1, 3) if what == 2 else (1, 3):
-            kv[what, i] = start(copy(of(src, what, i), dst.at[2 * i], (kv_s, kv_r), 5 * what + i, on_plane(i, 0)))
-        kv[what, 0] = start(copy(of(src, what, 0), dst.at[1], (fw_s, fw_r), 4 * what, sibling))
+            kv[what, i] = start(copy(of(src, what, i), dst.at[i, 0] if what == 2 else dst.at[2 * i], (kv_s, kv_r), 5 * what + i, on_plane(i, 0)))
+        kv[what, 0] = start(copy(of(src, what, 0), dst.at[0, 1] if what == 2 else dst.at[1], (fw_s, fw_r), 4 * what, sibling))
 
     def pass_on(what, partners):
         for i in partners:
@@ -179,7 +179,9 @@
 
     pass_on(1, (1, 3))
     relay(1)
-    pass_on(2, (1, 3, 2))
+    for i in (1, 3, 2):
+        arrived(kv[2, i])
+    kv[2, -1] = start(copy(marks.at[1:4, 0], marks.at[1:4, 1], (fw_s, fw_r), 9, sibling))
     pass_on(0, (2,))
 
     loaded(7)
@@ -190,9 +192,10 @@
 
     for n in (2, 3, 4):
         loaded(n)
-    for what in (0, 2):
-        for i in (0, -2, -1, -3):
-            arrived(kv[what, i])
+    for i in (0, -2, -1, -3):
+        arrived(kv[0, i])
+    for i in (0, -1):
+        arrived(kv[2, i])
     for cp in ag1:
         arrived(cp)
     token_f = token.astype(F32)
@@ -201,7 +204,7 @@
     for slot in range(8):
         i, d = slot // 2, slot % 2
         k = kb[slot]
-        flag = (mark[rows(x, 64), :] if slot == 0 else marks[slot]).astype(F32)
+        flag = (mark[rows(x, 64), :] if slot == 0 else marks[slot // 2, slot % 2]).astype(F32)
         s = lax.dot_general(q4, k, (((1,), (1,)), ((), ())), preferred_element_type=F32) * (LOG2E / HEAD**0.5)
         first = (chip(i, 0) * 2 + (c if d == 0 else 1 - c)) * 512
         for seg in range(2):
@@ -320,7 +323,7 @@
             pltpu.VMEM((8, 512, HEAD), BF16),
             pltpu.VMEM((8, 512, HEAD), BF16),
             pltpu.VMEM((256, SIDE), BF16),
-            pltpu.VMEM((8, 64, SIDE), BF16),
+            pltpu.VMEM((4, 2, 64, SIDE), BF16),
             pltpu.VMEM((HEADS * 64, 4096), F32),
             pltpu.VMEM((2, 64, 2 * HEAD + SIDE), BF16),
             pltpu.VMEM((2, 4, 16, 2 * HEAD + SIDE), BF16),

time: 49.3 us -> 49.3 us (level)
  no operation moved by 1% of the time
where the time goes in v5:
time: 49.3 us; the launch traced here: 49.2 us
  Pallas kernels  48.6 us (99%)
  local copies, waits for them, and re-layouts  0.61 us (1%)
    pallas_call x1, Pallas kernels, shards(): pl.pallas_call(kernel, out_shape=jax.ShapeDtypeStruct((32, 256), BF16), i...  48.6 us

profile of v5, /device:TPU:1, one launch (start us, length us, event | category | flops | bytes accessed | tf_op | source)
XLA Modules:
  0.0 49.2 jit_solution(11851420991655828146)
XLA Ops:
  0.0 48.6 %shard_map.82 = bf16[32,256]{1,0:T(8,128)(2,1)S(1)} custom-call(bf16[256,256]{1,0:T(8,128)(2,1)} %ts_hbm.1, bf16[256,1024]{1,0:T(8,128)(2,1)} %qw_hbm.1, f32[1,128]{1,0:T(1,128)} %bitcast.5, bf16[512,128]{1,0:T(8,128)(2,1)} %keys.1, bf16[512,128]{1,0:T(8,128)(2,1)} %values.1, s32[2,256]{1,0:T(2,128)} %bitcast.3, s32[1,256]{1,0:T(1,128)} %bitcast.4, ...), custom_call_target="tpu_custom_call" | custom-call | tf_op jit(solution)/shard_map/pallas_call | solution.py:303
  48.6 0.6 %copy.10 = bf16[32,256]{1,0:T(8,128)(2,1)} copy(bf16[32,256]{1,0:T(8,128)(2,1)S(1)} %shard_map.82) | data formatting | bytes 32768
